TPU v7x, 512 devices: a whole 4x8x8 slice. The times are simulated.
512 devices in a mesh: group: 64 (over z, x, core), tensor: 8 (over y).
Axes of the slice: x: 4, y: 8, z: 8, core: 2. Of those that a mesh axis runs over, the one named last changes fastest.
Arguments:
- hidden: bfloat16 [32768, 2048], P(('group', 'tensor')), may hold values from -6 to 6
- norm_gain: bfloat16 [2048], replicated, may hold values from 0.099609375 to 1.8984375
- q_weight: bfloat16 [2048, 3072], P(None, 'tensor'), may hold values from -0.125 to 0.125
- latent_down_weight: bfloat16 [2048, 512], P(None, 'tensor'), may hold values from -0.125 to 0.125
- kva_rope: bfloat16 [2048, 64], replicated, may hold values from -0.125 to 0.125
- latent_norm_scale: bfloat16 [512], replicated, may hold values from 0.099609375 to 1.8984375
- key_value_up_weight: bfloat16 [512, 4096], P(None, 'tensor'), may hold values from -0.25 to 0.25
- earlier_token_cache: bfloat16 [65536, 576], P('group'), may hold values from -2400 to 2400
- span_lens: int32 [64, 8], P('group'), may hold values from 1 to 256, 512 in all within a row
- prior_lens: int32 [64, 8], P('group'), may hold values from 2 to 128, as said below
- old_cache: bfloat16 [2, 524288, 576], P(None, ('group', 'tensor')), may hold values from -6 to 6
- block_slot: int32 [512, 64], P(('group', 'tensor')), may hold values from 0 to 63, each once within a row
Outputs:
- attn_out: bfloat16 [32768, 2048], P('group', 'tensor')
- new_cache: bfloat16 [2, 524288, 576], P(None, 'group', 'tensor')
Inputs may be any that keep to these rules, and one draw needn't show every extreme that they name: `prior_lens`: each row's values reach 128 in every group.
All inputs are finite; a program needn't handle non-finite values.
Results may differ from a plain program's by a relative error of at most 0.013.
The roundings to bfloat16 on the way count: a program that leaves them out, or rounds other values in their place, can miss the bound.
Values may be sent and summed in bfloat16 or wider, within the bound.
A program may use at most 128 MiB of HBM per device.

v0:
```python
import jax
import jax.numpy as jnp
from jax import lax
from jax.experimental import pallas as pl
from jax.experimental.pallas import tpu as pltpu
from jax.sharding import PartitionSpec as P

MESH = pl.DeviceIdType.MESH
BF = jnp.bfloat16
F32 = jnp.float32
EPS = 1e-06
LOG_BASE = 9.210340371976184
SCALE = 192 ** (-0.5)


def layer_kernel(slots_ref, span_ref, prior_ref, gain_ref, scale_ref,
                 hidden_ref, old_ref, qw_ref, latw_ref, kva_ref, up_ref, cache_ref,
                 attn_ref, new_ref,
                 own, arranged, landed, mid, hall, nrm, qw, wlk, up, cache, keys, vals, qcat, latall,
                 load_sem, ag_send, ag_recv, a_send, a_recv, b_send, b_recv, l_send, l_recv, out_sem):
    g = lax.axis_index("group")
    t = lax.axis_index("tensor")
    z, xc = g // 8, g % 8
    x, c = xc // 2, xc % 2
    right, left = lax.rem(t + 1, 8), lax.rem(t + 7, 8)

    def side(k):
        return lax.rem(x + k // 2, 4) * 2 + lax.rem(c + k % 2, 2)

    loads = [pltpu.make_async_copy(src, dst, load_sem.at[i]) for i, (src, dst) in enumerate([
        (old_ref, own), (hidden_ref, hall.at[t]), (up_ref, up), (cache_ref, cache),
        (latw_ref, wlk.at[0:64]), (kva_ref, wlk.at[64:128]), (qw_ref, qw)])]
    for load in loads:
        load.start()

    barrier = pltpu.get_barrier_semaphore()
    for k in range(1, 8):
        pl.semaphore_signal(barrier, inc=1, device_id=(z * 8 + side(k), t), device_id_type=MESH)

    def greet(k, carry):
        zz, tt = lax.rem(z + k // 8, 8), lax.rem(t + k % 8, 8)
        pl.semaphore_signal(barrier, inc=1, device_id=(zz * 8 + xc, tt), device_id_type=MESH)
        return carry

    lax.fori_loop(1, 64, greet, 0)
    pl.semaphore_wait(barrier, 70)

    def hop(way, step, half):
        owner = lax.rem(t + (8 - step if way == 0 else step), 8)
        rows = pl.ds(half * 32, 32)
        src = hidden_ref.at[rows] if step == 0 else hall.at[owner, rows]
        return pltpu.make_async_remote_copy(
            src_ref=src, dst_ref=hall.at[owner, rows],
            send_sem=ag_send.at[way, step, half], recv_sem=ag_recv.at[way, step, half],
            device_id=(g, right if way == 0 else left), device_id_type=MESH)

    hops = [[(w, s, h) for h in (0, 1) for w in (0, 1) if s < 3 or h == w] for s in range(4)]

    def pass_on(s):
        for w, _, h in hops[s]:
            hop(w, s, h).wait_recv()
            if s < 3 and (w, s + 1, h) in hops[s + 1]:
                hop(w, s + 1, h).start()

    for w, s, h in hops[0]:
        hop(w, s, h).start()

    slots = jnp.broadcast_to(slots_ref[...], (8, 64))
    spread = (lax.broadcasted_iota(jnp.int32, (64, 1024), 1) // 16
              == lax.broadcasted_iota(jnp.int32, (64, 1024), 0)).astype(BF)
    slot_of = jnp.dot(slots.astype(F32).astype(BF), spread, preferred_element_type=F32)[0:1]
    slot_of = jnp.broadcast_to(slot_of, (256, 1024)).astype(jnp.int32)
    place_of = lax.broadcasted_iota(jnp.int32, (256, 1024), 1) % 16
    lane = lax.broadcasted_iota(jnp.int32, (256, 1024), 0)

    def a_copy(layer, k):
        return pltpu.make_async_remote_copy(
            src_ref=arranged.at[side(k), layer], dst_ref=landed.at[xc, layer],
            send_sem=a_send.at[layer, k], recv_sem=a_recv.at[layer, k],
            device_id=(z * 8 + side(k), t), device_id_type=MESH)

    picks = []
    for pair in range(4):
        want = (lane % 128) // 16 * 8 + pair * 2 + lane // 128
        picks.append(((slot_of == want) & (place_of == lane % 16)).astype(BF))
    loads[0].wait()
    stay = []
    for layer in range(2):
        for pair in range(4):
            got = lax.dot_general(own[layer], picks[pair], (((1,), (1,)), ((), ())),
                                  preferred_element_type=F32).astype(BF)
            arranged[2 * pair, layer] = got[:, :128]
            arranged[2 * pair + 1, layer] = got[:, 128:]
        for k in (4, 5, 2, 6, 3, 7, 1):
            a_copy(layer, k).start()
        stay.append(pltpu.make_async_copy(arranged.at[xc, layer], landed.at[xc, layer], out_sem.at[layer]))
        stay[layer].start()

    gain = gain_ref[...].astype(F32)

    def norm_rows(owner):
        rows = hall[owner].astype(F32)
        mean_sq = jnp.mean(rows * rows, axis=-1, keepdims=True)
        nrm[owner] = (rows * lax.rsqrt(mean_sq + EPS) * gain).astype(BF)

    loads[1].wait()
    norm_rows(t)
    pass_on(0)
    for load in loads[2:4]:
        load.wait()
    up_t = jnp.transpose(up[...].astype(F32)).astype(BF)

    def expand(latent_t, cols):
        wide = jnp.dot(up_t, latent_t, preferred_element_type=F32).astype(BF)
        for head in range(2):
            keys[head, 0:128, cols] = wide[head * 256:head * 256 + 128]
            vals[head, :, cols] = wide[head * 256 + 128:head * 256 + 256]

    for part in range(2):
        cols = slice(part * 512, part * 512 + 512)
        expand(cache[0:512, cols], cols)
        for head in range(2):
            keys[head, 128:192, cols] = cache[512:576, cols]
            keys[head, 192:256, cols] = cache[512:576, cols]
    norm_rows(left)
    norm_rows(right)
    pass_on(1)

    spans = [span_ref[0, r] for r in range(8)]
    priors = [prior_ref[0, r] for r in range(8)]
    starts = [jnp.int32(0)]
    for r in range(7):
        starts.append(starts[r] + spans[r])

    def places(token):
        start, prior, request = jnp.zeros_like(token), jnp.zeros_like(token) + priors[0], jnp.zeros_like(token)
        for r in range(1, 8):
            inside = token >= starts[r]
            start = jnp.where(inside, starts[r], start)
            prior = jnp.where(inside, priors[r], prior)
            request = jnp.where(inside, r, request)
        return start, prior, request

    token = lax.broadcasted_iota(jnp.int32, (32, 512), 1)
    start, prior, _ = places(token)
    position = (prior + token - start).astype(F32)
    pair_of = lax.broadcasted_iota(jnp.int32, (32, 512), 0).astype(F32)
    angle = position * jnp.exp(pair_of * (-2.0 / 64 * LOG_BASE))
    cosine, sine = jnp.cos(angle), jnp.sin(angle)

    def rotate(rows):
        first, second = rows[0:32], rows[32:64]
        return [first * cosine - second * sine, second * cosine + first * sine]

    norm_rows(lax.rem(t + 6, 8))
    norm_rows(lax.rem(t + 2, 8))
    pass_on(2)
    norm_rows(lax.rem(t + 5, 8))
    norm_rows(lax.rem(t + 3, 8))
    pass_on(3)
    norm_rows(lax.rem(t + 4, 8))

    normed = nrm[...].reshape(512, 2048)
    for load in loads[4:6]:
        load.wait()
    small = lax.dot_general(wlk[...], normed, (((1,), (1,)), ((), ())), preferred_element_type=F32)
    latall[t] = small[0:64].astype(BF)
    rotary_new = jnp.concatenate(rotate(small[64:128]), axis=0).astype(BF)
    for head in range(2):
        keys[head, 128:192, 1024:1536] = rotary_new
        keys[head, 192:256, 1024:1536] = rotary_new

    def l_copy(k):
        return pltpu.make_async_remote_copy(
            src_ref=latall.at[t], dst_ref=latall.at[t],
            send_sem=l_send.at[k], recv_sem=l_recv.at[k],
            device_id=(g, lax.rem(t + k, 8)), device_id_type=MESH)

    for k in (4, 3, 5, 2, 6, 1, 7):
        l_copy(k).start()

    col = lax.broadcasted_iota(jnp.int32, (1024, 256), 1)
    row = lax.broadcasted_iota(jnp.int32, (1024, 256), 0)
    swaps = [(row == (col % 128) // 16 * 128 + (pair * 2 + col // 128) * 16 + col % 16).astype(BF)
             for pair in range(4)]
    place = pl.ds(pl.multiple_of((t * 8 + z) * 128, 128), 128)

    def b_copy(layer, dz, dt):
        zz, tt = lax.rem(z + dz, 8), lax.rem(t + dt, 8)
        return pltpu.make_async_remote_copy(
            src_ref=mid.at[zz, layer, tt], dst_ref=new_ref.at[layer, :, place],
            send_sem=b_send.at[layer, dz * 8 + dt], recv_sem=b_recv.at[layer, dz * 8 + dt],
            device_id=(zz * 8 + xc, tt), device_id_type=MESH)

    keeps = []
    for layer in range(2):
        stay[layer].wait()
        for k in range(1, 8):
            a_copy(layer, k).wait_recv()
        every = jnp.concatenate([landed[s, layer] for s in range(8)], axis=1)
        for pair in range(4):
            got = jnp.dot(every, swaps[pair], preferred_element_type=F32).astype(BF)
            for u in range(8):
                mid[2 * pair, layer, u] = got[u * 72:(u + 1) * 72, :128]
                mid[2 * pair + 1, layer, u] = got[u * 72:(u + 1) * 72, 128:]

        def go(i, carry):
            far = (i >= 12).astype(jnp.int32)
            p = 1 + i // 4
            q = lax.rem(i, 4) + far
            for dz, dt in ((p, q), (8 - p, lax.rem(8 - q, 8)), (q, 8 - p), (lax.rem(8 - q, 8), p)):
                b_copy(layer, dz, dt).start()
            return carry

        lax.fori_loop(0, 15, go, 0)
        for dz, dt in ((4, 0), (0, 4), (4, 4)):
            b_copy(layer, dz, dt).start()
        keep = pltpu.make_async_copy(mid.at[z, layer, t], new_ref.at[layer, :, place], out_sem.at[2 + layer])
        keep.start()
        keeps.append(keep)

    loads[6].wait()
    query = jnp.dot(normed, qw[...], preferred_element_type=F32)
    turned = jnp.transpose(jnp.concatenate([query[:, 128:192], query[:, 320:384]], axis=1))
    turned = jnp.transpose(jnp.concatenate(rotate(turned[0:64]) + rotate(turned[64:128]), axis=0))
    half = lax.broadcasted_iota(jnp.int32, (512, 128), 1) // 64
    for head in range(2):
        qcat[head, :, 0:128] = query[:, head * 192:head * 192 + 128].astype(BF)
        qcat[head, :, 128:256] = jnp.where(half == head, turned, 0.0).astype(BF)

    for k in range(1, 8):
        l_copy(k).wait_recv()
    latent = latall[...].reshape(512, 512).astype(F32)
    mean_sq = jnp.mean(latent * latent, axis=0, keepdims=True)
    scale = jnp.transpose(jnp.broadcast_to(scale_ref[...].astype(F32), (128, 512)))
    scale = jnp.concatenate([scale] * 4, axis=1)
    expand((latent * lax.rsqrt(mean_sq + EPS) * scale).astype(BF), slice(1024, 1536))

    def attend(block, carry):
        rows = pl.ds(pl.multiple_of(block * 128, 128), 128)
        mine = lax.broadcasted_iota(jnp.int32, (128, 1), 0) + block * 128
        start, prior, request = places(mine)
        key = lax.broadcasted_iota(jnp.int32, (128, 1536), 1)
        allowed = ((key >= request * 128) & (key < request * 128 + prior)) | (
            (key >= start + 1024) & (key <= mine + 1024))
        for head in range(2):
            scores = jnp.dot(qcat[head, rows, :], keys[head], preferred_element_type=F32) * SCALE
            scores = jnp.where(allowed, scores, -jnp.inf)
            weights = jnp.exp(scores - jnp.max(scores, axis=-1, keepdims=True))
            probs = (weights / jnp.sum(weights, axis=-1, keepdims=True)).astype(BF)
            mixed = lax.dot_general(probs, vals[head], (((1,), (1,)), ((), ())), preferred_element_type=F32)
            attn_ref[rows, head * 128:head * 128 + 128] = mixed.astype(BF)
        return carry

    lax.fori_loop(0, 4, attend, 0)

    for s in range(4):
        for w, _, h in hops[s]:
            hop(w, s, h).wait_send()
    for k in range(1, 8):
        l_copy(k).wait_send()
    for layer in range(2):
        keeps[layer].wait()
        for k in range(1, 8):
            a_copy(layer, k).wait_send()

        def end(k, carry):
            copy = b_copy(layer, k // 8, lax.rem(k, 8))
            copy.wait_send()
            copy.wait_recv()
            return carry

        lax.fori_loop(1, 64, end, 0)


def local(hidden, norm_gain, q_weight, latent_down_weight, kva_rope, latent_norm_scale,
          key_value_up_weight, earlier_token_cache, span_lens, prior_lens, old_cache, block_slot):
    whole = pl.BlockSpec(memory_space=pl.ANY)
    vmem = pl.BlockSpec(memory_space=pltpu.VMEM)
    smem = pl.BlockSpec(memory_space=pltpu.SMEM)
    dma = pltpu.SemaphoreType.DMA
    attn_out, moved = pl.pallas_call(
        layer_kernel,
        out_shape=(jax.ShapeDtypeStruct((512, 256), BF), jax.ShapeDtypeStruct((2, 72, 8192), BF)),
        in_specs=[vmem, smem, smem, vmem, vmem] + [whole] * 7,
        out_specs=(vmem, whole),
        scratch_shapes=[
            pltpu.VMEM((2, 576, 1024), BF),
            pltpu.VMEM((8, 2, 576, 128), BF),
            pltpu.VMEM((8, 2, 576, 128), BF),
            pltpu.VMEM((8, 2, 8, 72, 128), BF),
            pltpu.VMEM((8, 64, 2048), BF),
            pltpu.VMEM((8, 64, 2048), BF),
            pltpu.VMEM((2048, 384), BF),
            pltpu.VMEM((128, 2048), BF),
            pltpu.VMEM((512, 512), BF),
            pltpu.VMEM((576, 1024), BF),
            pltpu.VMEM((2, 256, 1536), BF),
            pltpu.VMEM((2, 128, 1536), BF),
            pltpu.VMEM((2, 512, 256), BF),
            pltpu.VMEM((8, 64, 512), BF),
            dma((7,)), dma((2, 4, 2)), dma((2, 4, 2)), dma((2, 8)), dma((2, 8)), dma((2, 64)), dma((2, 64)),
            dma((8,)), dma((8,)), dma((4,)),
        ],
        compiler_params=pltpu.CompilerParams(collective_id=0, has_side_effects=True, vmem_limit_bytes=56 << 20),
    )(
        block_slot, span_lens, prior_lens, norm_gain[None], latent_norm_scale[None],
        hidden, jnp.swapaxes(old_cache, 1, 2), q_weight, latent_down_weight.T, kva_rope.T,
        key_value_up_weight, earlier_token_cache.T,
    )
    return attn_out, jnp.swapaxes(moved, 1, 2)


def solution(mesh):
    in_specs = (
        P(("group", "tensor"), None),
        P(),
        P(None, "tensor"),
        P(None, "tensor"),
        P(),
        P(),
        P(None, "tensor"),
        P("group", None),
        P("group", None),
        P("group", None),
        P(None, ("group", "tensor"), None),
        P(("group", "tensor"), None),
    )
    out_specs = (P("group", "tensor"), P(None, "group", "tensor"))
    return jax.shard_map(local, mesh=mesh, in_specs=in_specs, out_specs=out_specs, check_vma=False)
```

profile of v0, /device:TPU:1, one launch (start us, length us, event | category | flops | bytes accessed | tf_op | source)
XLA Modules:
  0.0 116.8 jit_solution(3455564137057855495)
XLA Ops:
  0.6 1.3 %broadcast_in_dim.7.scale_ref = bf16[1,512]{1,0:T(2,128)(2,1)} reshape(bf16[512]{0:T(512)(128)(2,1)} %param.17) | data formatting | bytes 2048 | tf_op jit(solution)/shard_map/broadcast_in_dim | solution.py:307
  1.9 1.3 %broadcast_in_dim.6.gain_ref = bf16[1,2048]{1,0:T(2,128)(2,1)} reshape(bf16[2048]{0:T(1024)(128)(2,1)} %param.13) | data formatting | bytes 8192 | tf_op jit(solution)/shard_map/broadcast_in_dim | solution.py:307
  3.2 108.7 %shard_map.131 = (bf16[512,256]{1,0:T(8,128)(2,1)}, bf16[2,72,8192]{2,1,0:T(8,128)(2,1)}) custom-call(s32[1,64]{1,0:T(1,128)} %slots_ref.1, s32[1,8]{1,0:T(1,128)} %span_ref.1, s32[1,8]{1,0:T(1,128)} %prior_ref.1, bf16[1,2048]{1,0:T(2,128)(2,1)} %broadcast_in_dim.6.gain_ref, bf16[1,512]{1,0:T(2,128)(2,1)} %broadcast_in_dim.7.scale_ref, ...), custom_call_target="tpu_custom_call" | custom-call | tf_op jit(solution)/shard_map/pallas_call | solution.py:282
  111.9 1.7 %copy.16 = bf16[512,256]{1,0:T(8,128)(2,1)} copy(bf16[512,256]{1,0:T(8,128)(2,1)} %get-tuple-element.8) | data formatting | bytes 524288
  113.5 3.3 %copy.17 = bf16[2,8192,72]{1,2,0:T(8,128)(2,1)} copy(bf16[2,8192,72]{1,2,0:T(8,128)(2,1)} %bitcast.6) | data formatting | bytes 4718592
where the time goes:
time: 119 us; the launch traced here: 117 us
  Pallas kernels  109 us (92%)
  local copies, waits for them, and re-layouts  7.49 us (6%)
    pallas_call x1, Pallas kernels, local(): pl.pallas_call(layer_kernel, out_shape=(jax.ShapeDtypeStruct((512, 256),...  109 us
    unnamed x2, local copies, waits for them, and re-layouts  4.94 us

commit v1 on v0

--- a/solution.py
+++ b/solution.py
@@ -16,8 +16,8 @@
 def layer_kernel(slots_ref, span_ref, prior_ref, gain_ref, scale_ref,
                  hidden_ref, old_ref, qw_ref, latw_ref, kva_ref, up_ref, cache_ref,
                  attn_ref, new_ref,
-                 own, arranged, landed, mid, hall, nrm, qw, wlk, up, cache, keys, vals, qcat, latall,
-                 load_sem, ag_send, ag_recv, a_send, a_recv, b_send, b_recv, l_send, l_recv, out_sem):
+                 own, arranged, landed, mid, hall, nrm, qw, kva, up, cache, keys, vals, qcat, wall, pick, swap,
+                 load_sem, ag_send, ag_recv, a_send, a_recv, b_send, b_recv, w_send, w_recv, out_sem):
     g = lax.axis_index("group")
     t = lax.axis_index("tensor")
     z, xc = g // 8, g % 8
@@ -27,9 +27,10 @@
     def side(k):
         return lax.rem(x + k // 2, 4) * 2 + lax.rem(c + k % 2, 2)
 
+    piece = pl.ds(pl.multiple_of((z * 2 + c) * 128, 128), 128)
     loads = [pltpu.make_async_copy(src, dst, load_sem.at[i]) for i, (src, dst) in enumerate([
         (old_ref, own), (hidden_ref, hall.at[t]), (up_ref, up), (cache_ref, cache),
-        (latw_ref, wlk.at[0:64]), (kva_ref, wlk.at[64:128]), (qw_ref, qw)])]
+        (latw_ref.at[:, piece], wall.at[t, :, piece]), (kva_ref, kva), (qw_ref, qw)])]
     for load in loads:
         load.start()
 
@@ -65,47 +66,130 @@
     for w, s, h in hops[0]:
         hop(w, s, h).start()
 
+    def w_copy(stage, k):
+        if stage == 0:
+            peer, src, dst = (g, lax.rem(t + k, 8)), latw_ref.at[:, piece], wall.at[t, :, piece]
+        elif stage == 1:
+            peer, src, dst = (lax.rem(z + k, 8) * 8 + xc, t), wall.at[:, :, piece], wall.at[:, :, piece]
+        else:
+            cols = pl.ds(pl.multiple_of((lax.rem(z + 8 - k, 8) * 2 + c) * 128, 128), 128)
+            peer, src, dst = (z * 8 + side(1), t), wall.at[:, :, cols], wall.at[:, :, cols]
+        return pltpu.make_async_remote_copy(
+            src_ref=src, dst_ref=dst, send_sem=w_send.at[stage, k], recv_sem=w_recv.at[stage, k],
+            device_id=peer, device_id_type=MESH)
+
+    for k in (4, 3, 5, 2, 6, 1, 7):
+        w_copy(0, k).start()
+
     slots = jnp.broadcast_to(slots_ref[...], (8, 64))
     spread = (lax.broadcasted_iota(jnp.int32, (64, 1024), 1) // 16
               == lax.broadcasted_iota(jnp.int32, (64, 1024), 0)).astype(BF)
-    slot_of = jnp.dot(slots.astype(F32).astype(BF), spread, preferred_element_type=F32)[0:1]
-    slot_of = jnp.broadcast_to(slot_of, (256, 1024)).astype(jnp.int32)
-    place_of = lax.broadcasted_iota(jnp.int32, (256, 1024), 1) % 16
-    lane = lax.broadcasted_iota(jnp.int32, (256, 1024), 0)
+    slot_of = jnp.dot(slots.astype(F32).astype(BF), spread, preferred_element_type=F32)[0:1].astype(jnp.int32)
+    code_of = slot_of * 16 + lax.broadcasted_iota(jnp.int32, (1, 1024), 1) % 16
+    code_of = jnp.broadcast_to(code_of, (256, 1024))
+    lane = lax.broadcasted_iota(jnp.int32, (256, 1), 0)
+
+    seat = pl.ds(pl.multiple_of(xc * 128, 128), 128)
 
     def a_copy(layer, k):
         return pltpu.make_async_remote_copy(
-            src_ref=arranged.at[side(k), layer], dst_ref=landed.at[xc, layer],
+            src_ref=arranged.at[side(k), layer], dst_ref=landed.at[layer, :, seat],
             send_sem=a_send.at[layer, k], recv_sem=a_recv.at[layer, k],
             device_id=(z * 8 + side(k), t), device_id_type=MESH)
 
-    picks = []
-    for pair in range(4):
-        want = (lane % 128) // 16 * 8 + pair * 2 + lane // 128
-        picks.append(((slot_of == want) & (place_of == lane % 16)).astype(BF))
     loads[0].wait()
     stay = []
+    for pair in range(4):
+        want = ((lane % 128) // 16 * 8 + pair * 2 + lane // 128) * 16 + lane % 16
+        pick[pair] = (code_of == jnp.broadcast_to(want, (256, 1024))).astype(BF)
     for layer in range(2):
         for pair in range(4):
-            got = lax.dot_general(own[layer], picks[pair], (((1,), (1,)), ((), ())),
+            got = lax.dot_general(own[layer], pick[pair], (((1,), (1,)), ((), ())),
                                   preferred_element_type=F32).astype(BF)
             arranged[2 * pair, layer] = got[:, :128]
             arranged[2 * pair + 1, layer] = got[:, 128:]
         for k in (4, 5, 2, 6, 3, 7, 1):
             a_copy(layer, k).start()
-        stay.append(pltpu.make_async_copy(arranged.at[xc, layer], landed.at[xc, layer], out_sem.at[layer]))
+        stay.append(pltpu.make_async_copy(arranged.at[xc, layer], landed.at[layer, :, seat], out_sem.at[layer]))
         stay[layer].start()
-
-    gain = gain_ref[...].astype(F32)
+        if layer == 0:
+            pass_on(0)
+            loads[4].wait()
+            for k in range(1, 8):
+                w_copy(0, k).wait_recv()
+            for k in (4, 3, 5, 2, 6, 1, 7):
+                w_copy(1, k).start()
+
+    gain = gain_ref[...].reshape(1, 2048).astype(F32)
 
     def norm_rows(owner):
         rows = hall[owner].astype(F32)
         mean_sq = jnp.mean(rows * rows, axis=-1, keepdims=True)
         nrm[owner] = (rows * lax.rsqrt(mean_sq + EPS) * gain).astype(BF)
 
+    row = lax.broadcasted_iota(jnp.int32, (1024, 256), 0)
+    col = lax.broadcasted_iota(jnp.int32, (1, 256), 1)
+    for pair in range(4):
+        want = (col % 128) // 16 * 128 + (pair * 2 + col // 128) * 16 + col % 16
+        swap[pair] = (row == jnp.broadcast_to(want, (1024, 256))).astype(BF)
+    pass_on(1)
     loads[1].wait()
     norm_rows(t)
-    pass_on(0)
+    norm_rows(left)
+    norm_rows(right)
+    norm_rows(lax.rem(t + 6, 8))
+    norm_rows(lax.rem(t + 2, 8))
+    pass_on(2)
+
+    place = pl.ds(pl.multiple_of((t * 8 + z) * 128, 128), 128)
+
+    def b_copy(layer, dz, dt):
+        zz, tt = lax.rem(z + dz, 8), lax.rem(t + dt, 8)
+        return pltpu.make_async_remote_copy(
+            src_ref=mid.at[zz, layer, tt], dst_ref=new_ref.at[layer, :, place],
+            send_sem=b_send.at[layer, dz * 8 + dt], recv_sem=b_recv.at[layer, dz * 8 + dt],
+            device_id=(zz * 8 + xc, tt), device_id_type=MESH)
+
+    keeps = []
+
+    def send_layer(layer):
+        stay[layer].wait()
+        for k in range(1, 8):
+            a_copy(layer, k).wait_recv()
+        for pair in range(4):
+            got = jnp.dot(landed[layer], swap[pair], preferred_element_type=F32).astype(BF)
+            for u in range(8):
+                mid[2 * pair, layer, u] = got[u * 72:(u + 1) * 72, :128]
+                mid[2 * pair + 1, layer, u] = got[u * 72:(u + 1) * 72, 128:]
+
+        def go(i, carry):
+            far = (i >= 12).astype(jnp.int32)
+            p = 1 + i // 4
+            q = lax.rem(i, 4) + far
+            for dz, dt in ((p, q), (8 - p, lax.rem(8 - q, 8)), (q, 8 - p), (lax.rem(8 - q, 8), p)):
+                b_copy(layer, dz, dt).start()
+            return carry
+
+        lax.fori_loop(0, 15, go, 0)
+        for dz, dt in ((4, 0), (0, 4), (4, 4)):
+            b_copy(layer, dz, dt).start()
+        keep = pltpu.make_async_copy(mid.at[z, layer, t], new_ref.at[layer, :, place], out_sem.at[2 + layer])
+        keep.start()
+        keeps.append(keep)
+
+    send_layer(0)
+    norm_rows(lax.rem(t + 5, 8))
+    norm_rows(lax.rem(t + 3, 8))
+    pass_on(3)
+    norm_rows(lax.rem(t + 4, 8))
+
+    normed = nrm[...].reshape(512, 2048)
+    send_layer(1)
+    w_copy(2, 0).start()
+    for k in (1, 7, 2, 6, 3, 5, 4):
+        w_copy(1, k).wait_recv()
+        w_copy(2, k).start()
+
     for load in loads[2:4]:
         load.wait()
     up_t = jnp.transpose(up[...].astype(F32)).astype(BF)
@@ -122,9 +206,6 @@
         for head in range(2):
             keys[head, 128:192, cols] = cache[512:576, cols]
             keys[head, 192:256, cols] = cache[512:576, cols]
-    norm_rows(left)
-    norm_rows(right)
-    pass_on(1)
 
     spans = [span_ref[0, r] for r in range(8)]
     priors = [prior_ref[0, r] for r in range(8)]
@@ -152,72 +233,12 @@
         first, second = rows[0:32], rows[32:64]
         return [first * cosine - second * sine, second * cosine + first * sine]
 
-    norm_rows(lax.rem(t + 6, 8))
-    norm_rows(lax.rem(t + 2, 8))
-    pass_on(2)
-    norm_rows(lax.rem(t + 5, 8))
-    norm_rows(lax.rem(t + 3, 8))
-    pass_on(3)
-    norm_rows(lax.rem(t + 4, 8))
-
-    normed = nrm[...].reshape(512, 2048)
-    for load in loads[4:6]:
-        load.wait()
-    small = lax.dot_general(wlk[...], normed, (((1,), (1,)), ((), ())), preferred_element_type=F32)
-    latall[t] = small[0:64].astype(BF)
-    rotary_new = jnp.concatenate(rotate(small[64:128]), axis=0).astype(BF)
+    loads[5].wait()
+    rotary_new = lax.dot_general(kva[...], normed, (((1,), (1,)), ((), ())), preferred_element_type=F32)
+    rotary_new = jnp.concatenate(rotate(rotary_new), axis=0).astype(BF)
     for head in range(2):
         keys[head, 128:192, 1024:1536] = rotary_new
         keys[head, 192:256, 1024:1536] = rotary_new
-
-    def l_copy(k):
-        return pltpu.make_async_remote_copy(
-            src_ref=latall.at[t], dst_ref=latall.at[t],
-            send_sem=l_send.at[k], recv_sem=l_recv.at[k],
-            device_id=(g, lax.rem(t + k, 8)), device_id_type=MESH)
-
-    for k in (4, 3, 5, 2, 6, 1, 7):
-        l_copy(k).start()
-
-    col = lax.broadcasted_iota(jnp.int32, (1024, 256), 1)
-    row = lax.broadcasted_iota(jnp.int32, (1024, 256), 0)
-    swaps = [(row == (col % 128) // 16 * 128 + (pair * 2 + col // 128) * 16 + col % 16).astype(BF)
-             for pair in range(4)]
-    place = pl.ds(pl.multiple_of((t * 8 + z) * 128, 128), 128)
-
-    def b_copy(layer, dz, dt):
-        zz, tt = lax.rem(z + dz, 8), lax.rem(t + dt, 8)
-        return pltpu.make_async_remote_copy(
-            src_ref=mid.at[zz, layer, tt], dst_ref=new_ref.at[layer, :, place],
-            send_sem=b_send.at[layer, dz * 8 + dt], recv_sem=b_recv.at[layer, dz * 8 + dt],
-            device_id=(zz * 8 + xc, tt), device_id_type=MESH)
-
-    keeps = []
-    for layer in range(2):
-        stay[layer].wait()
-        for k in range(1, 8):
-            a_copy(layer, k).wait_recv()
-        every = jnp.concatenate([landed[s, layer] for s in range(8)], axis=1)
-        for pair in range(4):
-            got = jnp.dot(every, swaps[pair], preferred_element_type=F32).astype(BF)
-            for u in range(8):
-                mid[2 * pair, layer, u] = got[u * 72:(u + 1) * 72, :128]
-                mid[2 * pair + 1, layer, u] = got[u * 72:(u + 1) * 72, 128:]
-
-        def go(i, carry):
-            far = (i >= 12).astype(jnp.int32)
-            p = 1 + i // 4
-            q = lax.rem(i, 4) + far
-            for dz, dt in ((p, q), (8 - p, lax.rem(8 - q, 8)), (q, 8 - p), (lax.rem(8 - q, 8), p)):
-                b_copy(layer, dz, dt).start()
-            return carry
-
-        lax.fori_loop(0, 15, go, 0)
-        for dz, dt in ((4, 0), (0, 4), (4, 4)):
-            b_copy(layer, dz, dt).start()
-        keep = pltpu.make_async_copy(mid.at[z, layer, t], new_ref.at[layer, :, place], out_sem.at[2 + layer])
-        keep.start()
-        keeps.append(keep)
 
     loads[6].wait()
     query = jnp.dot(normed, qw[...], preferred_element_type=F32)
@@ -228,11 +249,12 @@
         qcat[head, :, 0:128] = query[:, head * 192:head * 192 + 128].astype(BF)
         qcat[head, :, 128:256] = jnp.where(half == head, turned, 0.0).astype(BF)
 
-    for k in range(1, 8):
-        l_copy(k).wait_recv()
-    latent = latall[...].reshape(512, 512).astype(F32)
+    for k in range(8):
+        w_copy(2, k).wait_recv()
+    latent = lax.dot_general(wall[...].reshape(512, 2048), normed, (((1,), (1,)), ((), ())),
+                             preferred_element_type=F32)
     mean_sq = jnp.mean(latent * latent, axis=0, keepdims=True)
-    scale = jnp.transpose(jnp.broadcast_to(scale_ref[...].astype(F32), (128, 512)))
+    scale = jnp.transpose(jnp.broadcast_to(scale_ref[...].reshape(1, 512).astype(F32), (128, 512)))
     scale = jnp.concatenate([scale] * 4, axis=1)
     expand((latent * lax.rsqrt(mean_sq + EPS) * scale).astype(BF), slice(1024, 1536))
 
@@ -257,8 +279,9 @@
     for s in range(4):
         for w, _, h in hops[s]:
             hop(w, s, h).wait_send()
-    for k in range(1, 8):
-        l_copy(k).wait_send()
+    for stage in range(3):
+        for k in range(1 if stage < 2 else 0, 8):
+            w_copy(stage, k).wait_send()
     for layer in range(2):
         keeps[layer].wait()
         for k in range(1, 8):
@@ -271,6 +294,23 @@
             return carry
 
         lax.fori_loop(1, 64, end, 0)
+
+
+def finish_kernel(attn_ref, new_ref, attn_out, new_out, attn_buf, new_buf, in_sem, out_sem):
+    pieces = [(attn_ref, attn_buf, attn_out)]
+    for layer in range(2):
+        for r in range(3):
+            rows = slice(24 * r, 24 * r + 24)
+            pieces.append((new_ref.at[layer, rows], new_buf.at[layer, rows], new_out.at[layer, rows]))
+    takes = [pltpu.make_async_copy(src, buf, in_sem.at[i]) for i, (src, buf, dst) in enumerate(pieces)]
+    puts = [pltpu.make_async_copy(buf, dst, out_sem.at[i]) for i, (src, buf, dst) in enumerate(pieces)]
+    for take in takes:
+        take.start()
+    for take, put in zip(takes, puts):
+        take.wait()
+        put.start()
+    for put in puts:
+        put.wait()
 
 
 def local(hidden, norm_gain, q_weight, latent_down_weight, kva_rope, latent_norm_scale,
@@ -287,27 +327,36 @@
         scratch_shapes=[
             pltpu.VMEM((2, 576, 1024), BF),
             pltpu.VMEM((8, 2, 576, 128), BF),
-            pltpu.VMEM((8, 2, 576, 128), BF),
+            pltpu.VMEM((2, 576, 1024), BF),
             pltpu.VMEM((8, 2, 8, 72, 128), BF),
             pltpu.VMEM((8, 64, 2048), BF),
             pltpu.VMEM((8, 64, 2048), BF),
             pltpu.VMEM((2048, 384), BF),
-            pltpu.VMEM((128, 2048), BF),
+            pltpu.VMEM((64, 2048), BF),
             pltpu.VMEM((512, 512), BF),
             pltpu.VMEM((576, 1024), BF),
             pltpu.VMEM((2, 256, 1536), BF),
             pltpu.VMEM((2, 128, 1536), BF),
             pltpu.VMEM((2, 512, 256), BF),
-            pltpu.VMEM((8, 64, 512), BF),
+            pltpu.VMEM((8, 64, 2048), BF),
+            pltpu.VMEM((4, 256, 1024), BF),
+            pltpu.VMEM((4, 1024, 256), BF),
             dma((7,)), dma((2, 4, 2)), dma((2, 4, 2)), dma((2, 8)), dma((2, 8)), dma((2, 64)), dma((2, 64)),
-            dma((8,)), dma((8,)), dma((4,)),
+            dma((3, 8)), dma((3, 8)), dma((4,)),
         ],
         compiler_params=pltpu.CompilerParams(collective_id=0, has_side_effects=True, vmem_limit_bytes=56 << 20),
     )(
-        block_slot, span_lens, prior_lens, norm_gain[None], latent_norm_scale[None],
+        block_slot, span_lens, prior_lens, norm_gain, latent_norm_scale,
         hidden, jnp.swapaxes(old_cache, 1, 2), q_weight, latent_down_weight.T, kva_rope.T,
         key_value_up_weight, earlier_token_cache.T,
     )
+    attn_out, moved = pl.pallas_call(
+        finish_kernel,
+        out_shape=(jax.ShapeDtypeStruct((512, 256), BF), jax.ShapeDtypeStruct((2, 72, 8192), BF)),
+        in_specs=[whole, whole],
+        out_specs=(whole, whole),
+        scratch_shapes=[pltpu.VMEM((512, 256), BF), pltpu.VMEM((2, 72, 8192), BF), dma((7,)), dma((7,))],
+    )(attn_out, moved)
     return attn_out, jnp.swapaxes(moved, 1, 2)
 
 

time: 119 us -> 119 us (level); the launches traced: 117 us -> 118 us
  Pallas kernels: 109 us -> 117 us
  local copies, waits for them, and re-layouts: 7.49 us -> 0 us
    pallas_call x1, Pallas kernels: 109 us -> 115 us  [local(): pl.pallas_call(layer_kernel, out_shape=(jax.ShapeDtypeStruct((512, 256),...]
    unnamed x2 -> x0, local copies, waits for them, and re-layouts: 4.94 us -> none
    pallas_call x0 -> x1, Pallas kernels: none -> 2.59 us  [local(): pl.pallas_call(finish_kernel, out_shape=(jax.ShapeDtypeStruct((512, 256),...]
    broadcast_in_dim x2 -> x0, local copies, waits for them, and re-layouts: 2.55 us -> none  [the longest x1 1.29 us: local(): norm_gain[None]]
where the time goes in v1:
time: 119 us; the launch traced here: 118 us
  Pallas kernels  117 us (98%)
    pallas_call x1, Pallas kernels, local(): pl.pallas_call(layer_kernel, out_shape=(jax.ShapeDtypeStruct((512, 256),...  115 us
    pallas_call x1, Pallas kernels, local(): pl.pallas_call(finish_kernel, out_shape=(jax.ShapeDtypeStruct((512, 256),...  2.59 us

profile of v1, /device:TPU:1, one launch (start us, length us, event | category | flops | bytes accessed | tf_op | source)
XLA Modules:
  0.0 118.0 jit_solution(17791761799862107937)
XLA Ops:
  0.6 114.8 %shard_map.131 = (bf16[512,256]{1,0:T(8,128)(2,1)}, bf16[2,72,8192]{2,1,0:T(8,128)(2,1)}) custom-call(s32[1,64]{1,0:T(1,128)} %slots_ref.1, s32[1,8]{1,0:T(1,128)} %span_ref.1, s32[1,8]{1,0:T(1,128)} %prior_ref.1, bf16[2048]{0:T(1024)(128)(2,1)} %gain_ref.1, bf16[512]{0:T(512)(128)(2,1)} %scale_ref.1, bf16[64,2048]{1,0:T(8,128)(2,1)} %hidden_ref.1, ...), custom_call_target="tpu_custom_call" | custom-call | tf_op jit(solution)/shard_map/pallas_call | solution.py:322
  115.4 2.6 %shard_map.132 = (bf16[512,256]{1,0:T(8,128)(2,1)}, bf16[2,72,8192]{2,1,0:T(8,128)(2,1)}) custom-call(bf16[512,256]{1,0:T(8,128)(2,1)} %get-tuple-element.6.attn_ref, bf16[2,72,8192]{2,1,0:T(8,128)(2,1)} %get-tuple-element.7.new_ref), custom_call_target="tpu_custom_call" | custom-call | tf_op jit(solution)/shard_map/pallas_call | solution.py:353

commit v2 on v1

--- a/solution.py
+++ b/solution.py
@@ -82,12 +82,13 @@
         w_copy(0, k).start()
 
     slots = jnp.broadcast_to(slots_ref[...], (8, 64))
-    spread = (lax.broadcasted_iota(jnp.int32, (64, 1024), 1) // 16
-              == lax.broadcasted_iota(jnp.int32, (64, 1024), 0)).astype(BF)
-    slot_of = jnp.dot(slots.astype(F32).astype(BF), spread, preferred_element_type=F32)[0:1].astype(jnp.int32)
-    code_of = slot_of * 16 + lax.broadcasted_iota(jnp.int32, (1, 1024), 1) % 16
-    code_of = jnp.broadcast_to(code_of, (256, 1024))
-    lane = lax.broadcasted_iota(jnp.int32, (256, 1), 0)
+    spread = (lax.broadcasted_iota(jnp.int32, (1024, 64), 0) // 16
+              == lax.broadcasted_iota(jnp.int32, (1024, 64), 1)).astype(BF)
+    slot_of = lax.dot_general(spread, slots.astype(F32).astype(BF), (((1,), (1,)), ((), ())),
+                              preferred_element_type=F32)[:, 0:1].astype(jnp.int32)
+    code_of = slot_of * 16 + lax.broadcasted_iota(jnp.int32, (1024, 1), 0) % 16
+    code_of = jnp.broadcast_to(code_of, (1024, 256))
+    lane = lax.broadcasted_iota(jnp.int32, (1, 256), 1)
 
     seat = pl.ds(pl.multiple_of(xc * 128, 128), 128)
 
@@ -101,11 +102,10 @@
     stay = []
     for pair in range(4):
         want = ((lane % 128) // 16 * 8 + pair * 2 + lane // 128) * 16 + lane % 16
-        pick[pair] = (code_of == jnp.broadcast_to(want, (256, 1024))).astype(BF)
+        pick[pair] = (code_of == jnp.broadcast_to(want, (1024, 256))).astype(BF)
     for layer in range(2):
         for pair in range(4):
-            got = lax.dot_general(own[layer], pick[pair], (((1,), (1,)), ((), ())),
-                                  preferred_element_type=F32).astype(BF)
+            got = jnp.dot(own[layer], pick[pair], preferred_element_type=F32).astype(BF)
             arranged[2 * pair, layer] = got[:, :128]
             arranged[2 * pair + 1, layer] = got[:, 128:]
         for k in (4, 5, 2, 6, 3, 7, 1):
@@ -180,16 +180,6 @@
     send_layer(0)
     norm_rows(lax.rem(t + 5, 8))
     norm_rows(lax.rem(t + 3, 8))
-    pass_on(3)
-    norm_rows(lax.rem(t + 4, 8))
-
-    normed = nrm[...].reshape(512, 2048)
-    send_layer(1)
-    w_copy(2, 0).start()
-    for k in (1, 7, 2, 6, 3, 5, 4):
-        w_copy(1, k).wait_recv()
-        w_copy(2, k).start()
-
     for load in loads[2:4]:
         load.wait()
     up_t = jnp.transpose(up[...].astype(F32)).astype(BF)
@@ -232,6 +222,17 @@
     def rotate(rows):
         first, second = rows[0:32], rows[32:64]
         return [first * cosine - second * sine, second * cosine + first * sine]
+
+    send_layer(1)
+
+    pass_on(3)
+    norm_rows(lax.rem(t + 4, 8))
+
+    normed = nrm[...].reshape(512, 2048)
+    w_copy(2, 0).start()
+    for k in (1, 7, 2, 6, 3, 5, 4):
+        w_copy(1, k).wait_recv()
+        w_copy(2, k).start()
 
     loads[5].wait()
     rotary_new = lax.dot_general(kva[...], normed, (((1,), (1,)), ((), ())), preferred_element_type=F32)
@@ -339,7 +340,7 @@
             pltpu.VMEM((2, 128, 1536), BF),
             pltpu.VMEM((2, 512, 256), BF),
             pltpu.VMEM((8, 64, 2048), BF),
-            pltpu.VMEM((4, 256, 1024), BF),
+            pltpu.VMEM((4, 1024, 256), BF),
             pltpu.VMEM((4, 1024, 256), BF),
             dma((7,)), dma((2, 4, 2)), dma((2, 4, 2)), dma((2, 8)), dma((2, 8)), dma((2, 64)), dma((2, 64)),
             dma((3, 8)), dma((3, 8)), dma((4,)),

time: 119 us -> 118 us (level)
  no operation moved by 1% of the time
where the time goes in v2:
time: 118 us
  Pallas kernels  117 us (99%)
    pallas_call x1, Pallas kernels, local(): pl.pallas_call(layer_kernel, out_shape=(jax.ShapeDtypeStruct((512, 256),...  115 us
    pallas_call x1, Pallas kernels, local(): pl.pallas_call(finish_kernel, out_shape=(jax.ShapeDtypeStruct((512, 256),...  2.59 us

profile of v2, /device:TPU:1, one launch (start us, length us, event | category | flops | bytes accessed | tf_op | source)
XLA Modules:
  0.0 118.0 jit_solution(6542439848034812392)
XLA Ops:
  0.6 114.7 %shard_map.131 = (bf16[512,256]{1,0:T(8,128)(2,1)}, bf16[2,72,8192]{2,1,0:T(8,128)(2,1)}) custom-call(s32[1,64]{1,0:T(1,128)} %slots_ref.1, s32[1,8]{1,0:T(1,128)} %span_ref.1, s32[1,8]{1,0:T(1,128)} %prior_ref.1, bf16[2048]{0:T(1024)(128)(2,1)} %gain_ref.1, bf16[512]{0:T(512)(128)(2,1)} %scale_ref.1, bf16[64,2048]{1,0:T(8,128)(2,1)} %hidden_ref.1, ...), custom_call_target="tpu_custom_call" | custom-call | tf_op jit(solution)/shard_map/pallas_call | solution.py:323
  115.4 2.6 %shard_map.132 = (bf16[512,256]{1,0:T(8,128)(2,1)}, bf16[2,72,8192]{2,1,0:T(8,128)(2,1)}) custom-call(bf16[512,256]{1,0:T(8,128)(2,1)} %get-tuple-element.6.attn_ref, bf16[2,72,8192]{2,1,0:T(8,128)(2,1)} %get-tuple-element.7.new_ref), custom_call_target="tpu_custom_call" | custom-call | tf_op jit(solution)/shard_map/pallas_call | solution.py:354
